TPU v7x, 32 devices: a whole 2x2x4 slice. The times are simulated.
32 devices in a mesh: dp: 8 (over y, x, core), seq: 4 (over z).
Axes of the slice: x: 2, y: 2, z: 4, core: 2. Of those that a mesh axis runs over, the one named last changes fastest.
Arguments:
- tokens: bfloat16 [8, 512, 6, 768], P('dp', 'seq'), may hold values from -6 to 6
- kind: int32 [8], P('dp'), may hold values from 0 to 1, as said below
- ln1_gain: float32 [768], replicated, may hold values from 0.1 to 1.9
- w_in: bfloat16 [768, 2304], replicated, may hold values from -0.21875 to 0.21875
- short_taps: float32 [3, 2304], replicated, may hold values from -3 to 3
- cond_taps: float32 [3, 768], replicated, may hold values from -3 to 3
- w_cond: bfloat16 [768, 768], replicated, may hold values from -0.21875 to 0.21875
- cond_bias: float32 [768], replicated, may hold values from -3 to 3
- w_out: bfloat16 [768, 768], replicated, may hold values from -0.21875 to 0.21875
- ln2_gain: float32 [768], replicated, may hold values from 0.1 to 1.9
- w_gate: bfloat16 [768, 3072], replicated, may hold values from -0.21875 to 0.21875
- w_up: bfloat16 [768, 3072], replicated, may hold values from -0.21875 to 0.21875
- w_down: bfloat16 [3072, 768], replicated, may hold values from -0.109375 to 0.109375
- cotangent: bfloat16 [8, 512, 6, 768], P('dp', 'seq'), may hold values from -6 to 6
Outputs:
- layer_out: bfloat16 [8, 512, 6, 768], P('dp', 'seq')
- grad_tokens: bfloat16 [8, 512, 6, 768], P('dp', 'seq')
- grad_ln1: float32 [768], P('seq')
- grad_w_in: float32 [768, 2304], P('seq')
- grad_short_taps: float32 [3, 2304], P(None, 'seq')
- grad_cond_taps: float32 [3, 768], P(None, 'seq')
- grad_w_cond: float32 [768, 768], P('seq')
- grad_cond_bias: float32 [768], P('seq')
- grad_w_out: float32 [768, 768], P('seq')
- grad_ln2: float32 [768], P('seq')
- grad_gate: float32 [768, 3072], P('seq')
- grad_up: float32 [768, 3072], P('seq')
- grad_down: float32 [3072, 768], P('seq')
Inputs may be any that keep to these rules, and one draw needn't show every extreme that they name: Exactly 4 groups have kind 1.
All inputs are finite; a program needn't handle non-finite values.
Results may differ from a plain program's by a relative error of at most 0.017.
Values may be sent and summed in bfloat16 or wider, within the bound.
A program may use at most 256 MiB of HBM per device.

v0:
```python
import math
import jax
import jax.numpy as jnp
from jax import lax
from jax.sharding import PartitionSpec as P

highest = lax.Precision.HIGHEST
epsilon = 1e-05


def from_behind(value, axis, by):
    peers = lax.axis_size(axis)
    pairs = [(i, i + by) for i in range(peers) if 0 <= i + by < peers]
    return lax.ppermute(value, axis, pairs)


def norm_rows(values, scale_gain):
    row_mean = jnp.mean(values, axis=-1, keepdims=True)
    centered = values - row_mean
    scale_inv = lax.rsqrt(jnp.mean(centered * centered, axis=-1, keepdims=True) + epsilon)
    normed = centered * scale_inv
    return (normed * scale_gain, normed, scale_inv)


def norm_back(grad_out, normed, scale_inv, scale_gain):
    grad_gain = jnp.sum(grad_out * normed, axis=0)
    grad_normed = grad_out * scale_gain
    inner_mean = jnp.mean(grad_normed, axis=-1, keepdims=True)
    inner_cross = jnp.mean(grad_normed * normed, axis=-1, keepdims=True)
    return (scale_inv * (grad_normed - inner_mean - normed * inner_cross), grad_gain)


def wave_tables(freq_ids, time_ids, span_len):
    fold_freq = freq_ids[:, None] % span_len
    fold_time = time_ids[None, :] % span_len
    same_block = (freq_ids[:, None] // span_len == time_ids[None, :] // span_len).astype(
        jnp.float32
    )
    phase_index = fold_freq * fold_time % span_len
    phase_angle = phase_index.astype(jnp.float32) * (2.0 * math.pi) / span_len.astype(jnp.float32)
    return (jnp.cos(phase_angle) * same_block, jnp.sin(phase_angle) * same_block)


def conv_forward(extended, taps):
    return taps[0] * extended[2:] + taps[1] * extended[1:-1] + taps[2] * extended[:-2]


def conv_backward(grad_out, extended, taps, long_flag):
    count_rows = grad_out.shape[0]
    zero_pad = jnp.zeros((2,) + grad_out.shape[1:], jnp.float32)
    padded = jnp.concatenate([grad_out, zero_pad], axis=0)
    grad_local = (
        taps[0] * padded[:count_rows] + taps[1] * padded[1 : count_rows + 1] + taps[2] * padded[2:]
    )
    grad_rim = (
        jnp.stack([taps[2] * grad_out[0], taps[1] * grad_out[0] + taps[2] * grad_out[1]])
        * long_flag
    )
    grad_taps = jnp.stack(
        [
            jnp.sum(grad_out * extended[2:], axis=(0, 1)),
            jnp.sum(grad_out * extended[1:-1], axis=(0, 1)),
            jnp.sum(grad_out * extended[:-2], axis=(0, 1)),
        ]
    )
    return (grad_local, grad_rim, grad_taps)


def on_device(
    tokens,
    kind,
    ln1_gain,
    w_in,
    short_taps,
    cond_taps,
    w_cond,
    cond_bias,
    w_out,
    ln2_gain,
    w_gate,
    w_up,
    w_down,
    cotangent,
):
    piece_rows = tokens.shape[1]
    slot_count = tokens.shape[2]
    model_width = tokens.shape[3]
    flat_rows = piece_rows * slot_count
    seq_count = lax.axis_size("seq")
    seq_rank = lax.axis_index("seq")
    is_long = kind[0]
    long_flag = is_long.astype(jnp.float32)
    span_len = jnp.where(is_long == 1, piece_rows * seq_count, piece_rows).astype(jnp.int32)
    span_float = span_len.astype(jnp.float32)
    freq_ids = seq_rank * piece_rows + jnp.arange(piece_rows, dtype=jnp.int32)
    token_rows = tokens.reshape(flat_rows, model_width).astype(jnp.float32)
    normed_one, unit_one, inv_one = norm_rows(token_rows, ln1_gain)
    normed_one_low = normed_one.astype(jnp.bfloat16)
    projected = jnp.dot(normed_one_low, w_in, preferred_element_type=jnp.float32)
    proj_low = projected.astype(jnp.bfloat16).reshape(piece_rows, slot_count, 3 * model_width)
    proj_f = proj_low.astype(jnp.float32)
    rim_proj = from_behind(proj_low[piece_rows - 2 :], "seq", 1).astype(jnp.float32) * long_flag
    extended_proj = jnp.concatenate([rim_proj, proj_f], axis=0)
    conv_out = conv_forward(extended_proj, short_taps)
    query_conv = conv_out[:, :, :model_width]
    key_conv = conv_out[:, :, model_width : 2 * model_width]
    value_low = conv_out[:, :, 2 * model_width :].astype(jnp.bfloat16)
    value_f = value_low.astype(jnp.float32)
    rim_value = from_behind(value_low[piece_rows - 2 :], "seq", 1).astype(jnp.float32) * long_flag
    extended_value = jnp.concatenate([rim_value, value_f], axis=0)
    cond_low = conv_forward(extended_value, cond_taps).astype(jnp.bfloat16)
    signal_low = (key_conv * value_f).astype(jnp.bfloat16)
    sig_piece = lax.all_gather(signal_low, "seq", axis=0, tiled=True).astype(jnp.float32)
    cond_piece = lax.all_gather(cond_low, "seq", axis=0, tiled=True).astype(jnp.float32)
    time_ids = jnp.arange(sig_piece.shape[0], dtype=jnp.int32)
    cos_table, sin_table = wave_tables(freq_ids, time_ids, span_len)
    sig_cos = jnp.einsum("ft,tsd->fsd", cos_table, sig_piece, precision=highest)
    sig_sin = jnp.einsum("ft,tsd->fsd", sin_table, sig_piece, precision=highest)
    cond_cos = jnp.einsum("ft,tsd->fsd", cos_table, cond_piece, precision=highest)
    cond_sin = jnp.einsum("ft,tsd->fsd", sin_table, cond_piece, precision=highest)
    power_spec = (cond_cos * cond_cos + cond_sin * cond_sin) / span_float
    features_low = jnp.log1p(power_spec).astype(jnp.bfloat16).reshape(flat_rows, model_width)
    pre_tanh = jnp.dot(features_low, w_cond, preferred_element_type=jnp.float32) + cond_bias
    tanh_value = jnp.tanh(pre_tanh).reshape(piece_rows, slot_count, model_width)
    spectral_gain = 1.0 + tanh_value
    gained_cos = spectral_gain * sig_cos
    gained_sin = spectral_gain * sig_sin
    time_ids = jnp.arange(piece_rows * lax.axis_size("seq"), dtype=jnp.int32)
    cos_table, sin_table = wave_tables(freq_ids, time_ids, span_len)
    term = jnp.einsum("ft,fsd->tsd", cos_table, gained_cos, precision=highest) + jnp.einsum(
        "ft,fsd->tsd", sin_table, gained_sin, precision=highest
    )
    filtered = lax.psum_scatter(
        (term / span_float).astype(jnp.bfloat16), "seq", scatter_dimension=0, tiled=True
    ).astype(jnp.float32)
    mixed_low = (query_conv * filtered).astype(jnp.bfloat16).reshape(flat_rows, model_width)
    hidden_one = token_rows + jnp.dot(mixed_low, w_out, preferred_element_type=jnp.float32)
    normed_two, unit_two, inv_two = norm_rows(hidden_one, ln2_gain)
    normed_two_low = normed_two.astype(jnp.bfloat16)
    gate_pre = jnp.dot(normed_two_low, w_gate, preferred_element_type=jnp.float32)
    up_proj = jnp.dot(normed_two_low, w_up, preferred_element_type=jnp.float32)
    gate_sig = jax.nn.sigmoid(gate_pre)
    gate_act = gate_pre * gate_sig
    hidden_act = (gate_act * up_proj).astype(jnp.bfloat16)
    layer_rows = hidden_one + jnp.dot(hidden_act, w_down, preferred_element_type=jnp.float32)
    layer_out = layer_rows.astype(jnp.bfloat16).reshape(tokens.shape)
    cot_rows = cotangent.reshape(flat_rows, model_width)
    grad_down = jnp.einsum("nf,nd->fd", hidden_act, cot_rows, preferred_element_type=jnp.float32)
    grad_act = jnp.einsum("nd,fd->nf", cot_rows, w_down, preferred_element_type=jnp.float32)
    grad_gate_pre = (grad_act * up_proj * gate_sig * (1.0 + gate_pre * (1.0 - gate_sig))).astype(
        jnp.bfloat16
    )
    grad_up_proj = (grad_act * gate_act).astype(jnp.bfloat16)
    grad_gate = jnp.einsum(
        "nd,nf->df", normed_two_low, grad_gate_pre, preferred_element_type=jnp.float32
    )
    grad_up = jnp.einsum(
        "nd,nf->df", normed_two_low, grad_up_proj, preferred_element_type=jnp.float32
    )
    grad_normed_two = jnp.einsum(
        "nf,df->nd", grad_gate_pre, w_gate, preferred_element_type=jnp.float32
    ) + jnp.einsum("nf,df->nd", grad_up_proj, w_up, preferred_element_type=jnp.float32)
    grad_hidden_part, grad_ln2 = norm_back(grad_normed_two, unit_two, inv_two, ln2_gain)
    grad_hidden = cot_rows.astype(jnp.float32) + grad_hidden_part
    grad_mix_low = grad_hidden.astype(jnp.bfloat16)
    grad_w_out = jnp.einsum(
        "nd,ne->de", mixed_low, grad_mix_low, preferred_element_type=jnp.float32
    )
    grad_mixed = jnp.einsum(
        "ne,de->nd", grad_mix_low, w_out, preferred_element_type=jnp.float32
    ).reshape(piece_rows, slot_count, model_width)
    grad_query = grad_mixed * filtered
    grad_filtered_low = (grad_mixed * query_conv).astype(jnp.bfloat16)
    grad_piece = lax.all_gather(grad_filtered_low, "seq", axis=0, tiled=True).astype(jnp.float32)
    time_ids = jnp.arange(grad_piece.shape[0], dtype=jnp.int32)
    cos_table, sin_table = wave_tables(freq_ids, time_ids, span_len)
    back_cos = jnp.einsum("ft,tsd->fsd", cos_table, grad_piece, precision=highest)
    back_sin = jnp.einsum("ft,tsd->fsd", sin_table, grad_piece, precision=highest)
    back_cos = back_cos / span_float
    back_sin = back_sin / span_float
    grad_gain_spec = back_cos * sig_cos + back_sin * sig_sin
    grad_sig_cos = spectral_gain * back_cos
    grad_sig_sin = spectral_gain * back_sin
    grad_pre_low = (
        (grad_gain_spec * (1.0 - tanh_value * tanh_value))
        .astype(jnp.bfloat16)
        .reshape(flat_rows, model_width)
    )
    grad_w_cond = jnp.einsum(
        "nc,nd->cd", features_low, grad_pre_low, preferred_element_type=jnp.float32
    )
    grad_cond_bias = jnp.sum(grad_pre_low.astype(jnp.float32), axis=0)
    grad_features = jnp.einsum(
        "nd,cd->nc", grad_pre_low, w_cond, preferred_element_type=jnp.float32
    ).reshape(piece_rows, slot_count, model_width)
    grad_power = grad_features / (1.0 + power_spec)
    grad_cond_cos = 2.0 * cond_cos * grad_power / span_float
    grad_cond_sin = 2.0 * cond_sin * grad_power / span_float
    time_ids = jnp.arange(piece_rows * lax.axis_size("seq"), dtype=jnp.int32)
    cos_table, sin_table = wave_tables(freq_ids, time_ids, span_len)
    signal_term = jnp.einsum(
        "ft,fsd->tsd", cos_table, grad_sig_cos, precision=highest
    ) + jnp.einsum("ft,fsd->tsd", sin_table, grad_sig_sin, precision=highest)
    cond_term = jnp.einsum("ft,fsd->tsd", cos_table, grad_cond_cos, precision=highest) + jnp.einsum(
        "ft,fsd->tsd", sin_table, grad_cond_sin, precision=highest
    )
    source_grads = lax.psum_scatter(
        jnp.concatenate([signal_term, cond_term], axis=2).astype(jnp.bfloat16),
        "seq",
        scatter_dimension=0,
        tiled=True,
    ).astype(jnp.float32)
    grad_signal = source_grads[:, :, :model_width]
    grad_cond = source_grads[:, :, model_width:]
    grad_value_cond, grad_value_rim, grad_cond_taps = conv_backward(
        grad_cond, extended_value, cond_taps, long_flag
    )
    grad_value = grad_signal * key_conv + grad_value_cond
    grad_key = grad_signal * value_f
    value_back = from_behind(grad_value_rim.astype(jnp.bfloat16), "seq", -1).astype(
        grad_value_rim.dtype
    )
    grad_value = jnp.concatenate(
        [grad_value[: piece_rows - 2], grad_value[piece_rows - 2 :] + value_back], axis=0
    )
    grad_conv = jnp.concatenate([grad_query, grad_key, grad_value], axis=2)
    grad_proj_local, grad_proj_rim, grad_short_taps = conv_backward(
        grad_conv, extended_proj, short_taps, long_flag
    )
    proj_back = from_behind(grad_proj_rim.astype(jnp.bfloat16), "seq", -1).astype(
        grad_proj_rim.dtype
    )
    grad_proj = jnp.concatenate(
        [grad_proj_local[: piece_rows - 2], grad_proj_local[piece_rows - 2 :] + proj_back], axis=0
    )
    grad_proj_low = grad_proj.astype(jnp.bfloat16).reshape(flat_rows, 3 * model_width)
    grad_w_in = jnp.einsum(
        "nd,ne->de", normed_one_low, grad_proj_low, preferred_element_type=jnp.float32
    )
    grad_normed_one = jnp.einsum(
        "ne,de->nd", grad_proj_low, w_in, preferred_element_type=jnp.float32
    )
    grad_token_part, grad_ln1 = norm_back(grad_normed_one, unit_one, inv_one, ln1_gain)
    grad_tokens = (grad_hidden + grad_token_part).astype(jnp.bfloat16).reshape(tokens.shape)
    whole_sums = lax.psum(
        (
            grad_ln1,
            grad_w_in,
            grad_short_taps,
            grad_cond_taps,
            grad_w_cond,
            grad_cond_bias,
            grad_w_out,
            grad_ln2,
            grad_gate,
            grad_up,
            grad_down,
        ),
        ("dp", "seq"),
    )
    seq_dims = (0, 0, 1, 1, 0, 0, 0, 0, 0, 0, 0)
    summed = tuple(
        (
            lax.dynamic_slice_in_dim(
                whole_sum,
                seq_rank * (whole_sum.shape[axis_dim] // seq_count),
                whole_sum.shape[axis_dim] // seq_count,
                axis_dim,
            )
            for whole_sum, axis_dim in zip(whole_sums, seq_dims)
        )
    )
    return (
        layer_out,
        grad_tokens,
        summed[0],
        summed[1],
        summed[2],
        summed[3],
        summed[4],
        summed[5],
        summed[6],
        summed[7],
        summed[8],
        summed[9],
        summed[10],
    )


def solution(mesh):
    return jax.shard_map(
        on_device,
        mesh=mesh,
        in_specs=(
            P("dp", "seq", None, None),
            P("dp"),
            P(),
            P(),
            P(),
            P(),
            P(),
            P(),
            P(),
            P(),
            P(),
            P(),
            P(),
            P("dp", "seq", None, None),
        ),
        out_specs=(
            P("dp", "seq", None, None),
            P("dp", "seq", None, None),
            P("seq"),
            P("seq", None),
            P(None, "seq"),
            P(None, "seq"),
            P("seq", None),
            P("seq"),
            P("seq", None),
            P("seq"),
            P("seq", None),
            P("seq", None),
            P("seq", None),
        ),
        check_vma=False,
    )
```

profile of v0, /device:TPU:0, one launch (start us, length us, event | category | flops | bytes accessed | tf_op | source)
XLA Modules:
  0.0 1427.0 jit_solution(9233570854723160421)
XLA Ops:
  12.5 3.9 reshape.284
  19.1 5.5 convolution_convert_fusion
  30.1 5.5 collective-permute-start
  38.7 6.8 reshape.285
  45.5 6.0 copy.77
  63.7 89.3 %all-gather.4.cloned.1.call-done = bf16[512,6,768]{2,0,1:T(8,128)(2,1)} async-done(((bf16[128,6,768]{2,0,1:T(8,128)(2,1)}), bf16[512,6,768]{2,0,1:T(8,128)(2,1)}) %all-gather.4.cloned.1.call-update) | async-done | bytes 4718608 | tf_op jit(solution)/shard_map/all_gather | solution.py:114
  153.0 8.0 fusion.64
  161.0 8.2 log-plus-one_convert_fusion
  175.3 5.0 multiply_subtract_fusion
  183.9 59.2 %all-gather.6.cloned.1.call-done = bf16[512,6,768]{2,0,1:T(8,128)(2,1)} async-done(((bf16[128,6,768]{2,0,1:T(8,128)(2,1)}), bf16[512,6,768]{2,0,1:T(8,128)(2,1)}) %all-gather.6.cloned.1.call-update) | async-done | bytes 4718608 | tf_op jit(solution)/shard_map/all_gather | solution.py:113
  243.1 7.8 fusion.62
  251.0 11.7 fusion.26
  262.7 5.5 fusion.54
  269.6 14.8 %divide_convert_fusion = bf16[512,6,768]{2,0,1:T(8,128)(2,1)} fusion(f32[512,6,768]{2,0,1:T(8,128)S(1)} %fusion.26, f32[]{:T(128)S(6)} %convert_element_type.160, f32[128,6,768]{2,0,1:T(8,128)S(1)} %fusion.54, f32[128,6,768]{2,1,0:T(8,128)S(1)} %copy-done.2, s32[]{:T(128)S(6)} %select_n.103, s32[512]{0:T(512)S(1)} %get-tuple-element.107, ...), kind=kOutput, calls=%fused_computation.8 | convolution fusion | flops 3632332800 | bytes 18879496 | tf_op jit(solution)/shard_map/ft,fsd->tsd/dot_general | solution.py:130
  291.1 77.2 %reduce-scatter.3.cloned.1.call-done = bf16[128,6,768]{2,0,1:T(8,128)(2,1)} async-done(((bf16[512,6,768]{2,0,1:T(8,128)(2,1)}), bf16[128,6,768]{2,0,1:T(8,128)(2,1)}) %reduce-scatter.3.cloned.1.call-update) | async-done | bytes 1179664 | tf_op jit(solution)/shard_map/reduce_scatter | solution.py:133
  380.3 9.2 fusion.142
  389.5 6.2 fusion.143
  395.8 17.3 %multiply_convert_fusion = (bf16[768,3072]{1,0:T(8,128)(2,1)}, bf16[768,3072]{1,0:T(8,128)(2,1)}, bf16[768,3072]{1,0:T(8,128)(2,1)}) fusion(f32[768,3072]{1,0:T(8,128)} %fusion.142, f32[768,3072]{1,0:T(8,128)} %fusion.143, bf16[768,768]{1,0:T(8,128)(2,1)S(1)} %copy-done.31, bf16[3072,768]{1,0:T(8,128)(2,1)} %param.26), kind=kOutput, calls=%fused_computation.3 | convolution fusion | flops 3659268096 | bytes 38928384 | tf_op jit(solution)/shard_map/nd,fd->nf/dot_general | solution.py:149
  413.1 7.7 fusion.144
  420.9 7.3 multiply_reduce_fusion.2
  436.8 5.7 convert_multiply_fusion
  446.3 86.3 %all-gather.8.cloned.1.call-done = bf16[512,6,768]{2,0,1:T(8,128)(2,1)} async-done(((bf16[128,6,768]{2,0,1:T(8,128)(2,1)}), bf16[512,6,768]{2,0,1:T(8,128)(2,1)}) %all-gather.8.cloned.1.call-update) | async-done | bytes 4718608 | tf_op jit(solution)/shard_map/all_gather | solution.py:174
  532.6 7.9 convolution_divide_fusion.1
  540.6 11.6 fusion.23
  552.3 9.2 convert_reduce_fusion
  561.5 4.3 add_divide_fusion.1
  565.7 11.2 fusion.18
  577.0 15.4 %add_convert_fusion = bf16[512,6,768]{2,0,1:T(8,128)(2,1)} fusion(f32[512,6,768]{2,0,1:T(8,128)S(1)} %fusion.18, f32[128,6,768]{2,0,1:T(8,128)S(1)} %add_divide_fusion.1, f32[128,6,768]{2,0,1:T(8,128)} %get-tuple-element.101, f32[]{:T(128)S(6)} %convert_element_type.160, s32[]{:T(128)S(6)} %select_n.103, s32[512]{0:T(512)S(1)} %get-tuple-element.107, ...), kind=kOutput, calls=%fused_computation.1 | convolution fusion | flops 3631153152 | bytes 18879496 | tf_op jit(solution)/shard_map/ft,fsd->tsd/dot_general | solution.py:204
  592.3 15.3 %add_convert_fusion.1 = bf16[512,6,768]{2,0,1:T(8,128)(2,1)S(1)} fusion(f32[512,6,768]{2,0,1:T(8,128)S(1)} %fusion.23, f32[128,6,768]{2,0,1:T(8,128)} %get-tuple-element.105, f32[128,6,768]{2,1,0:T(8,128)S(1)} %copy-done.3, f32[]{:T(128)S(6)} %convert_element_type.160, s32[]{:T(128)S(6)} %select_n.103, s32[512]{0:T(512)S(1)} %get-tuple-element.107, ...), kind=kOutput, calls=%fused_computation.2 | convolution fusion | flops 3629973504 | bytes 18879496 | tf_op jit(solution)/shard_map/ft,fsd->tsd/dot_general | solution.py:203
  607.6 4.4 pad_maximum_fusion
  619.9 4.7 fusion.41
  624.6 8.8 fusion.146
  633.5 6.3 fusion.147
  639.8 6.3 fusion.148
  648.8 123.1 %reduce-scatter.5.cloned.1.call-done = bf16[128,6,1536]{2,0,1:T(8,128)(2,1)} async-done(((bf16[512,6,1536]{2,0,1:T(8,128)(2,1)}), bf16[128,6,1536]{2,0,1:T(8,128)(2,1)}) %reduce-scatter.5.cloned.1.call-update) | async-done | bytes 2359312 | tf_op jit(solution)/shard_map/reduce_scatter | solution.py:207
  776.2 4.2 multiply_reduce_fusion.4
  780.8 4.6 multiply_reduce_fusion.1
  792.7 4.1 copy.96
  796.8 6.6 convert_element_type.184
  803.4 8.2 fusion.145
  811.7 4.9 copy.98
  816.6 10.0 add_convert_fusion.3
  832.5 4.1 concatenate.42
  836.5 4.8 copy.99
  841.3 3.9 concatenate.43
  858.6 4.9 fusion.6
  876.4 44.4 %all-reduce.2 = (f32[768]{0:T(1024)}, f32[3,2304]{1,0:T(4,128)}, f32[3,768]{1,0:T(4,128)}, f32[768]{0:T(1024)}, f32[768]{0:T(1024)}) all-reduce(f32[768]{0:T(1024)} %get-tuple-element.58, f32[3,2304]{1,0:T(4,128)} %pad_maximum_fusion.4, f32[3,768]{1,0:T(4,128)S(1)} %copy-done.56, ...), channel_id=1, replica_groups=mesh['dp'=8,'seq'=4] {'dp','seq'}, use_global_device_ids=true, to_apply=%region_11.12 | all-reduce | flops 11520 | bytes 92160 | tf_op jit(solution)/shard_map/psum | solution.py:245
  927.5 476.0 %all-reduce.6.cloned.1.call-done = (f32[768,2304]{1,0:T(8,128)}, f32[768,768]{1,0:T(8,128)}, f32[768,768]{1,0:T(8,128)}, f32[768,3072]{1,0:T(8,128)}, f32[768,3072]{1,0:T(8,128)}, /*index=5*/f32[3072,768]{1,0:T(8,128)}) async-done(((f32[768,2304]{1,0:T(8,128)}, f32[768,768]{1,0:T(8,128)}, f32[768,768]{1,0:T(8,128)}, f32[768,3072]{1,0:T(8,128)}, f32[768,3072]{1,0:T(8,128)}, ...) | async-done | bytes 40108048 | tf_op jit(solution)/shard_map/psum | solution.py:245
  (277 shorter events, 147.6 us)
Async XLA Ops:
  7.2 11.9 copy-start
  7.2 145.8 %all-gather.4.cloned.1.call-start = ((), (), s32[]{:S(2)}) async-start(), calls=%async_computation.2 | async-start | bytes 5898240 | tf_op jit(solution)/shard_map/all_gather | solution.py:114
  12.5 6.6 copy-start.63
  16.4 8.2 copy-start.57
  18.1 6.5 copy-start.65
  30.1 22.0 %collective-permute-start = (bf16[2,6,2304]{2,0,1:T(2,128)(2,1)}, bf16[2,6,2304]{2,0,1:T(2,128)(2,1)}, u32[]{:S(2)}, u32[]{:S(2)}) collective-permute-start(bf16[2,6,2304]{2,0,1:T(2,128)(2,1)} %copy.78), channel_id=1, source_target_pairs={{0,1},{1,2},{2,3},{4,5},{5,6},{6,7},{8,9},{9,10},{10,11},{12,13},{... | collective-permute-start | bytes 165896 | tf_op jit(solution)/shard_map/ppermute | solution.py:14
  37.2 15.8 %copy-start.44 = (f32[2304]{0:T(1024)}, f32[2304]{0:T(1024)S(1)}, u32[]{:S(2)}) copy-start(f32[2304]{0:T(1024)S(1)} %get-tuple-element.64) | copy-start | bytes 27652
  38.7 21.7 %copy-start.52 = (f32[768]{0:T(1024)}, f32[768]{0:T(1024)S(1)}, u32[]{:S(2)}) copy-start(f32[768]{0:T(1024)S(1)} %get-tuple-element.67) | copy-start | bytes 9220
  45.5 7.6 copy-start.46
  45.5 7.6 copy-start.48
  55.8 6.7 copy-start.4
  55.9 4.5 collective-permute-start.1
  62.5 180.6 %all-gather.6.cloned.1.call-start = ((), (), s32[]{:S(2)}) async-start(), calls=%async_computation.3 | async-start | bytes 5898240 | tf_op jit(solution)/shard_map/all_gather | solution.py:113
  63.2 305.1 %reduce-scatter.3.cloned.1.call-start = ((), (), s32[]{:S(2)}) async-start(), calls=%async_computation.4 | async-start | bytes 5898240 | tf_op jit(solution)/shard_map/reduce_scatter | solution.py:133
  153.0 8.0 copy-start.33
  161.0 8.2 copy-start.27
  243.1 7.8 copy-start.2
  243.1 19.6 %slice-start.2 = ((s8[4718592]{0:T(1024)(128)(4,1)}), s8[4194304]{0:T(1024)(128)(4,1)S(1)}, s32[]{:S(2)}) async-start(s8[4718592]{0:T(1024)(128)(4,1)} %bitcast.76), calls=%async_computation.10 | async-start | bytes 8388608
  251.0 11.7 copy-start.7
  251.0 11.7 slice-start.3
  284.5 248.1 %all-gather.8.cloned.1.call-start = ((), (), s32[]{:S(2)}) async-start(), calls=%async_computation.5 | async-start | bytes 5898240 | tf_op jit(solution)/shard_map/all_gather | solution.py:174
  379.2 49.0 %copy-start.5 = (f32[768,768]{1,0:T(8,128)}, f32[768,768]{1,0:T(8,128)S(1)}, u32[]{:S(2)}) copy-start(f32[768,768]{1,0:T(8,128)S(1)} %get-tuple-element.103) | copy-start | bytes 7077892
  379.9 9.6 slice-start.8
  380.2 9.3 copy-start.22
  380.3 9.3 slice-start.9
  389.5 6.3 copy-start.31
  413.1 7.8 copy-start.34
  442.5 329.4 %reduce-scatter.5.cloned.1.call-start = ((), (), s32[]{:S(2)}) async-start(), calls=%async_computation.6 | async-start | bytes 11796480 | tf_op jit(solution)/shard_map/reduce_scatter | solution.py:207
  532.6 8.0 copy-start.3
  532.6 19.6 %slice-start.4 = ((s8[4718592]{0:T(1024)(128)(4,1)}), s8[4194304]{0:T(1024)(128)(4,1)S(1)}, s32[]{:S(2)}) async-start(s8[4718592]{0:T(1024)(128)(4,1)} %bitcast.78), calls=%async_computation.12 | async-start | bytes 8388608
  540.5 11.7 copy-start.8
  540.6 11.7 copy-start.24
  540.6 11.7 copy-start.26
  540.6 11.7 slice-start.5
  552.3 9.2 copy-start.28
  592.3 15.3 %copy-start.18 = (bf16[512,6,768]{2,0,1:T(8,128)(2,1)S(1)}, bf16[512,6,768]{2,0,1:T(8,128)(2,1)}, u32[]{:S(2)}) copy-start(bf16[512,6,768]{2,0,1:T(8,128)(2,1)} %add_convert_fusion) | copy-start | bytes 14155780
  612.0 791.5 %all-reduce.6.cloned.1.call-start = ((), (), s32[]{:S(2)}) async-start(), calls=%async_computation.7 | async-start | bytes 80216064 | tf_op jit(solution)/shard_map/psum | solution.py:245
  619.9 13.5 slice-start.6
  624.6 8.8 slice-start.7
  624.6 15.2 %slice-start.10 = ((s8[4718592]{0:T(1024)(128)(4,1)}), s8[4194304]{0:T(1024)(128)(4,1)S(1)}, s32[]{:S(2)}) async-start(s8[4718592]{0:T(1024)(128)(4,1)} %bitcast.84), calls=%async_computation.18 | async-start | bytes 8388608
  633.5 6.3 copy-start.32
  633.5 6.3 slice-start.11
  639.8 6.4 copy-start.36
  639.8 6.4 copy-start.38
  648.8 125.6 %copy-start.53 = (f32[768]{0:T(1024)S(1)}, f32[768]{0:T(1024)}, u32[]{:S(2)}) copy-start(f32[768]{0:T(1024)} %copy-done.52) | copy-start | bytes 9220
  648.8 125.6 %copy-start.55 = (f32[768]{0:T(1024)S(1)}, f32[768]{0:T(1024)}, u32[]{:S(2)}) copy-start(f32[768]{0:T(1024)} %get-tuple-element.68) | copy-start | bytes 9220
  774.5 5.9 collective-permute-start.2
  785.6 6.8 collective-permute-start.3
  (45 other events, 172.8 us)
Sparse Core Ops, SparseCore 0:
  62.6 90.3 all-gather.3
  155.2 87.9 all-gather.5
  284.6 83.6 reduce-scatter.2
  442.6 89.9 all-gather.7
  612.1 159.7 reduce-scatter.4
  811.8 591.6 all-reduce.5
where the time goes:
time: 1440 us; the launch traced here: 1430 us
  waiting for transfers between devices  916 us (64%)
  matrix products  246 us (17%)
  local copies, waits for them, and re-layouts  146 us (10%)
  other arithmetic  46.6 us (3%)
  blocking collectives  44.4 us (3%)
  between operations  16.2 us (1%)
    psum x1, waiting for transfers between devices, on_device(): lax.psum((grad_ln1, grad_w_in, grad_short_taps, grad_cond_taps, grad_w_co...  476 us
    reduce_scatter x1, waiting for transfers between devices, on_device(): lax.psum_scatter(jnp.concatenate([signal_term, cond_term], axis=2).astype...  123 us
    all_gather x1, waiting for transfers between devices, on_device(): lax.all_gather(cond_low, 'seq', axis=0, tiled=True).astype(jnp.float32)  89.3 us
    all_gather x1, waiting for transfers between devices, on_device(): lax.all_gather(grad_filtered_low, 'seq', axis=0, tiled=True)  86.3 us
    reduce_scatter x1, waiting for transfers between devices, on_device(): lax.psum_scatter((term / span_float).astype(jnp.bfloat16), 'seq', scatter...  77.2 us
    all_gather x1, waiting for transfers between devices, on_device(): lax.all_gather(signal_low, 'seq', axis=0, tiled=True).astype(jnp.float32)  59.2 us
    psum x1, blocking collectives, on_device(): lax.psum((grad_ln1, grad_w_in, grad_short_taps, grad_cond_taps, grad_w_co...  44.4 us
  transfers between devices with their start and end apart: 10, of which 8 were waited for; matrix products, arithmetic and copies ran while one was open for 12% of the time, Pallas kernels for 0%

commit v1 on v0

--- a/solution.py
+++ b/solution.py
@@ -6,6 +6,18 @@
 
 highest = lax.Precision.HIGHEST
 epsilon = 1e-05
+
+
+def doubled_up(x, axis, dim):
+    ways, here = (lax.axis_size(axis), lax.axis_index(axis))
+    grown, reach = (x, 1)
+    while reach < ways:
+        theirs = lax.ppermute(grown, axis, [(d, d ^ reach) for d in range(ways)])
+        mine_first = jnp.concatenate([grown, theirs], axis=dim)
+        theirs_first = jnp.concatenate([theirs, grown], axis=dim)
+        grown = jnp.where(here & reach == 0, mine_first, theirs_first)
+        reach = 2 * reach
+    return grown
 
 
 def from_behind(value, axis, by):
@@ -111,7 +123,7 @@
     cond_low = conv_forward(extended_value, cond_taps).astype(jnp.bfloat16)
     signal_low = (key_conv * value_f).astype(jnp.bfloat16)
     sig_piece = lax.all_gather(signal_low, "seq", axis=0, tiled=True).astype(jnp.float32)
-    cond_piece = lax.all_gather(cond_low, "seq", axis=0, tiled=True).astype(jnp.float32)
+    cond_piece = doubled_up(cond_low, "seq", 0).astype(jnp.float32)
     time_ids = jnp.arange(sig_piece.shape[0], dtype=jnp.int32)
     cos_table, sin_table = wave_tables(freq_ids, time_ids, span_len)
     sig_cos = jnp.einsum("ft,tsd->fsd", cos_table, sig_piece, precision=highest)

time: 1440 us -> 1490 us (1.035)
  waiting for transfers between devices: 916 us -> 957 us
    ppermute x0 -> x2, waiting for transfers between devices: none -> 189 us  [doubled_up(): theirs = lax.ppermute(grown, axis, [(d, d ^ reach) for d in range(ways)])]
    all_gather x1 -> x0, waiting for transfers between devices: 89.3 us -> none  [on_device(): lax.all_gather(cond_low, 'seq', axis=0, tiled=True).astype(jnp.float32)]
    all_gather x1, waiting for transfers between devices: 59.2 us -> 0.01 us  [on_device(): lax.all_gather(signal_low, 'seq', axis=0, tiled=True).astype(jnp.float32)]
  transfers between devices with their start and end apart: 10 -> 11, of which waited for: 8 -> 8; matrix products, arithmetic and copies ran while one was open for 12% -> 12% of each run, Pallas kernels for 0% -> 0%
where the time goes in v1:
time: 1490 us; the launch traced here: 1480 us
  waiting for transfers between devices  957 us (64%)
  matrix products  254 us (17%)
  local copies, waits for them, and re-layouts  146 us (10%)
  other arithmetic  50.8 us (3%)
  blocking collectives  44.4 us (3%)
  between operations  15.8 us (1%)
    psum x1, waiting for transfers between devices, on_device(): lax.psum((grad_ln1, grad_w_in, grad_short_taps, grad_cond_taps, grad_w_co...  476 us
    ppermute x2, waiting for transfers between devices, doubled_up(): theirs = lax.ppermute(grown, axis, [(d, d ^ reach) for d in range(ways)])  189 us
    reduce_scatter x1, waiting for transfers between devices, on_device(): lax.psum_scatter(jnp.concatenate([signal_term, cond_term], axis=2).astype...  123 us
    all_gather x1, waiting for transfers between devices, on_device(): lax.all_gather(grad_filtered_low, 'seq', axis=0, tiled=True)  86.3 us
    reduce_scatter x1, waiting for transfers between devices, on_device(): lax.psum_scatter((term / span_float).astype(jnp.bfloat16), 'seq', scatter...  77.7 us
    psum x1, blocking collectives, on_device(): lax.psum((grad_ln1, grad_w_in, grad_short_taps, grad_cond_taps, grad_w_co...  44.4 us
  transfers between devices with their start and end apart: 11, of which 8 were waited for; matrix products, arithmetic and copies ran while one was open for 12% of the time, Pallas kernels for 0%

profile of v1, /device:TPU:0, one launch (start us, length us, event | category | flops | bytes accessed | tf_op | source)
XLA Modules:
  0.0 1482.0 jit_solution(1089705478494966883)
XLA Ops:
  19.1 5.5 convolution_convert_fusion
  30.1 5.5 collective-permute-start
  38.7 6.8 reshape.285
  45.5 6.0 copy.77
  64.9 73.6 %collective-permute-done.2 = bf16[128,6,768]{2,0,1:T(8,128)(2,1)} collective-permute-done((bf16[128,6,768]{2,0,1:T(8,128)(2,1)}, bf16[128,6,768]{2,0,1:T(8,128)(2,1)}, u32[]{:S(2)}, u32[]{:S(2)}) %collective-permute-start.2) | collective-permute-done | bytes 1179680 | tf_op jit(solution)/shard_map/ppermute | solution.py:15
  138.5 4.2 maximum_select_fusion.1
  143.7 115.9 %collective-permute-done.3 = bf16[256,6,768]{2,0,1:T(8,128)(2,1)} collective-permute-done((bf16[256,6,768]{2,0,1:T(8,128)(2,1)}, bf16[256,6,768]{2,0,1:T(8,128)(2,1)}, u32[]{:S(2)}, u32[]{:S(2)}) %collective-permute-start.3) | collective-permute-done | bytes 2359328 | tf_op jit(solution)/shard_map/ppermute | solution.py:15
  259.6 10.0 fusion.38
  269.7 13.6 log-plus-one_convert_fusion
  289.3 5.0 multiply_subtract_fusion
  297.8 7.8 fusion.63
  305.7 11.7 fusion.26
  317.4 5.5 fusion.56
  324.3 14.8 divide_convert_fusion
  345.8 77.7 %reduce-scatter.3.cloned.1.call-done = bf16[128,6,768]{2,0,1:T(8,128)(2,1)} async-done(((bf16[512,6,768]{2,0,1:T(8,128)(2,1)}), bf16[128,6,768]{2,0,1:T(8,128)(2,1)}) %reduce-scatter.3.cloned.1.call-update) | async-done | bytes 1179664 | tf_op jit(solution)/shard_map/reduce_scatter | solution.py:145
  435.5 9.2 fusion.144
  444.8 6.3 fusion.145
  451.1 17.3 %multiply_convert_fusion = (bf16[768,3072]{1,0:T(8,128)(2,1)}, bf16[768,3072]{1,0:T(8,128)(2,1)}, bf16[768,3072]{1,0:T(8,128)(2,1)}) fusion(f32[768,3072]{1,0:T(8,128)} %fusion.144, f32[768,3072]{1,0:T(8,128)} %fusion.145, bf16[768,768]{1,0:T(8,128)(2,1)S(1)} %copy-done.28, bf16[3072,768]{1,0:T(8,128)(2,1)} %param.26), kind=kOutput, calls=%fused_computation.3 | convolution fusion | flops 3659268096 | bytes 38928384 | tf_op jit(solution)/shard_map/nd,fd->nf/dot_general | solution.py:161
  468.5 7.7 fusion.146
  476.2 7.3 multiply_reduce_fusion.2
  492.2 5.7 convert_multiply_fusion
  501.7 86.3 %all-gather.5.cloned.1.call-done = bf16[512,6,768]{2,0,1:T(8,128)(2,1)} async-done(((bf16[128,6,768]{2,0,1:T(8,128)(2,1)}), bf16[512,6,768]{2,0,1:T(8,128)(2,1)}) %all-gather.5.cloned.1.call-update) | async-done | bytes 4718608 | tf_op jit(solution)/shard_map/all_gather | solution.py:186
  588.0 7.9 convolution_divide_fusion.1
  596.0 11.6 fusion.23
  607.7 9.2 convert_reduce_fusion
  616.8 4.2 add_divide_fusion.1
  621.1 11.2 fusion.18
  632.3 15.3 %add_convert_fusion = bf16[512,6,768]{2,0,1:T(8,128)(2,1)} fusion(f32[512,6,768]{2,0,1:T(8,128)S(1)} %fusion.18, f32[128,6,768]{2,0,1:T(8,128)S(1)} %add_divide_fusion.1, f32[128,6,768]{2,0,1:T(8,128)} %get-tuple-element.101, f32[]{:T(128)S(6)} %convert_element_type.160, s32[]{:T(128)S(6)} %select_n.119, s32[512]{0:T(512)S(1)} %get-tuple-element.107, ...), kind=kOutput, calls=%fused_computation.1 | convolution fusion | flops 3631153152 | bytes 18879496 | tf_op jit(solution)/shard_map/ft,fsd->tsd/dot_general | solution.py:216
  647.7 15.3 %add_convert_fusion.1 = bf16[512,6,768]{2,0,1:T(8,128)(2,1)S(1)} fusion(f32[512,6,768]{2,0,1:T(8,128)S(1)} %fusion.23, f32[128,6,768]{2,0,1:T(8,128)} %get-tuple-element.105, f32[128,6,768]{2,1,0:T(8,128)S(1)} %copy-done.3, f32[]{:T(128)S(6)} %convert_element_type.160, s32[]{:T(128)S(6)} %select_n.119, s32[512]{0:T(512)S(1)} %get-tuple-element.107, ...), kind=kOutput, calls=%fused_computation.2 | convolution fusion | flops 3629973504 | bytes 18879496 | tf_op jit(solution)/shard_map/ft,fsd->tsd/dot_general | solution.py:215
  662.9 4.4 pad_maximum_fusion
  675.3 4.7 fusion.43
  679.9 8.8 fusion.148
  688.8 6.4 fusion.149
  695.3 6.4 fusion.150
  704.3 123.0 %reduce-scatter.5.cloned.1.call-done = bf16[128,6,1536]{2,0,1:T(8,128)(2,1)} async-done(((bf16[512,6,1536]{2,0,1:T(8,128)(2,1)}), bf16[128,6,1536]{2,0,1:T(8,128)(2,1)}) %reduce-scatter.5.cloned.1.call-update) | async-done | bytes 2359312 | tf_op jit(solution)/shard_map/reduce_scatter | solution.py:219
  831.5 4.2 multiply_reduce_fusion.4
  836.1 4.6 multiply_reduce_fusion.1
  848.0 4.1 copy.96
  852.1 6.6 convert_element_type.184
  858.7 8.3 fusion.147
  867.0 4.9 copy.98
  871.9 10.0 add_convert_fusion.3
  887.8 4.1 concatenate.58
  891.9 4.8 copy.99
  896.7 3.9 concatenate.59
  914.0 4.9 fusion.6
  931.8 44.4 %all-reduce.2 = (f32[768]{0:T(1024)}, f32[3,2304]{1,0:T(4,128)}, f32[3,768]{1,0:T(4,128)}, f32[768]{0:T(1024)}, f32[768]{0:T(1024)}) all-reduce(f32[768]{0:T(1024)} %get-tuple-element.58, f32[3,2304]{1,0:T(4,128)} %pad_maximum_fusion.4, f32[3,768]{1,0:T(4,128)S(1)} %copy-done.55, ...), channel_id=1, replica_groups=mesh['dp'=8,'seq'=4] {'dp','seq'}, use_global_device_ids=true, to_apply=%region_11.12 | all-reduce | flops 11520 | bytes 92160 | tf_op jit(solution)/shard_map/psum | solution.py:257
  982.8 476.0 %all-reduce.6.cloned.1.call-done = (f32[768,2304]{1,0:T(8,128)}, f32[768,768]{1,0:T(8,128)}, f32[768,768]{1,0:T(8,128)}, f32[768,3072]{1,0:T(8,128)}, f32[768,3072]{1,0:T(8,128)}, /*index=5*/f32[3072,768]{1,0:T(8,128)}) async-done(((f32[768,2304]{1,0:T(8,128)}, f32[768,768]{1,0:T(8,128)}, f32[768,768]{1,0:T(8,128)}, f32[768,3072]{1,0:T(8,128)}, f32[768,3072]{1,0:T(8,128)}, ...) | async-done | bytes 40108048 | tf_op jit(solution)/shard_map/psum | solution.py:257
  (277 shorter events, 153.6 us)
Async XLA Ops:
  7.2 11.9 copy-start
  7.2 290.6 %all-gather.3.cloned.1.call-start = ((), (), s32[]{:S(2)}) async-start(), calls=%async_computation.2 | async-start | bytes 5898240 | tf_op jit(solution)/shard_map/all_gather | solution.py:125
  12.5 6.6 copy-start.62
  16.4 8.2 copy-start.56
  18.1 6.5 copy-start.64
  30.1 22.0 %collective-permute-start = (bf16[2,6,2304]{2,0,1:T(2,128)(2,1)}, bf16[2,6,2304]{2,0,1:T(2,128)(2,1)}, u32[]{:S(2)}, u32[]{:S(2)}) collective-permute-start(bf16[2,6,2304]{2,0,1:T(2,128)(2,1)} %copy.78), channel_id=1, source_target_pairs={{0,1},{1,2},{2,3},{4,5},{5,6},{6,7},{8,9},{9,10},{10,11},{12,13},{... | collective-permute-start | bytes 165896 | tf_op jit(solution)/shard_map/ppermute | solution.py:26
  37.2 15.8 %copy-start.43 = (f32[2304]{0:T(1024)}, f32[2304]{0:T(1024)S(1)}, u32[]{:S(2)}) copy-start(f32[2304]{0:T(1024)S(1)} %get-tuple-element.64) | copy-start | bytes 27652
  38.7 21.7 %copy-start.51 = (f32[768]{0:T(1024)}, f32[768]{0:T(1024)S(1)}, u32[]{:S(2)}) copy-start(f32[768]{0:T(1024)S(1)} %get-tuple-element.67) | copy-start | bytes 9220
  45.5 7.6 copy-start.45
  45.5 7.6 copy-start.47
  55.8 6.7 copy-start.4
  55.9 4.5 collective-permute-start.1
  62.5 361.0 %reduce-scatter.3.cloned.1.call-start = ((), (), s32[]{:S(2)}) async-start(), calls=%async_computation.3 | async-start | bytes 5898240 | tf_op jit(solution)/shard_map/reduce_scatter | solution.py:145
  62.5 75.9 %collective-permute-start.2 = (bf16[128,6,768]{2,0,1:T(8,128)(2,1)}, bf16[128,6,768]{2,0,1:T(8,128)(2,1)}, u32[]{:S(2)}, u32[]{:S(2)}) collective-permute-start(bf16[128,6,768]{2,0,1:T(8,128)(2,1)} %get-tuple-element.94), channel_id=1, source_target_pairs={{0,1},{1,0},{2,3},{3,2},{4,5},{5,4},{6,7},{7,6},{8,9},{9,8},{10,11... | collective-permute-start | bytes 3538952 | tf_op jit(solution)/shard_map/ppermute | solution.py:15
  142.7 116.9 %collective-permute-start.3 = (bf16[256,6,768]{2,0,1:T(8,128)(2,1)}, bf16[256,6,768]{2,0,1:T(8,128)(2,1)}, u32[]{:S(2)}, u32[]{:S(2)}) collective-permute-start(bf16[256,6,768]{2,0,1:T(8,128)(2,1)} %maximum_select_fusion.1), channel_id=1, source_target_pairs={{0,2},{1,3},{2,0},{3,1},{4,6},{5,7},{6,4},{7,5},{8,10},{9,11},{10,... | collective-permute-start | bytes 7077896 | tf_op jit(solution)/shard_map/ppermute | solution.py:15
  269.6 13.6 copy-start.33
  297.8 7.9 copy-start.2
  297.8 19.6 %slice-start.2 = ((s8[4718592]{0:T(1024)(128)(4,1)}), s8[4194304]{0:T(1024)(128)(4,1)S(1)}, s32[]{:S(2)}) async-start(s8[4718592]{0:T(1024)(128)(4,1)} %bitcast.74), calls=%async_computation.9 | async-start | bytes 8388608
  305.7 11.7 copy-start.7
  305.7 11.7 slice-start.3
  339.2 248.8 %all-gather.5.cloned.1.call-start = ((), (), s32[]{:S(2)}) async-start(), calls=%async_computation.4 | async-start | bytes 5898240 | tf_op jit(solution)/shard_map/all_gather | solution.py:186
  434.4 49.1 %copy-start.5 = (f32[768,768]{1,0:T(8,128)}, f32[768,768]{1,0:T(8,128)S(1)}, u32[]{:S(2)}) copy-start(f32[768,768]{1,0:T(8,128)S(1)} %get-tuple-element.103) | copy-start | bytes 7077892
  435.1 9.6 slice-start.8
  435.5 9.3 copy-start.22
  435.5 9.3 slice-start.9
  444.8 6.3 copy-start.28
  468.5 7.8 copy-start.30
  497.9 329.3 %reduce-scatter.5.cloned.1.call-start = ((), (), s32[]{:S(2)}) async-start(), calls=%async_computation.5 | async-start | bytes 11796480 | tf_op jit(solution)/shard_map/reduce_scatter | solution.py:219
  588.0 8.0 copy-start.3
  588.0 19.6 %slice-start.4 = ((s8[4718592]{0:T(1024)(128)(4,1)}), s8[4194304]{0:T(1024)(128)(4,1)S(1)}, s32[]{:S(2)}) async-start(s8[4718592]{0:T(1024)(128)(4,1)} %bitcast.76), calls=%async_computation.11 | async-start | bytes 8388608
  595.9 11.7 copy-start.8
  595.9 11.7 copy-start.24
  595.9 11.7 copy-start.26
  595.9 11.7 slice-start.5
  607.7 9.2 copy-start.32
  647.7 15.3 %copy-start.18 = (bf16[512,6,768]{2,0,1:T(8,128)(2,1)S(1)}, bf16[512,6,768]{2,0,1:T(8,128)(2,1)}, u32[]{:S(2)}) copy-start(bf16[512,6,768]{2,0,1:T(8,128)(2,1)} %add_convert_fusion) | copy-start | bytes 14155780
  667.3 791.5 %all-reduce.6.cloned.1.call-start = ((), (), s32[]{:S(2)}) async-start(), calls=%async_computation.6 | async-start | bytes 80216064 | tf_op jit(solution)/shard_map/psum | solution.py:257
  675.2 13.5 slice-start.6
  679.9 8.9 slice-start.7
  679.9 15.3 %slice-start.10 = ((s8[4718592]{0:T(1024)(128)(4,1)}), s8[4194304]{0:T(1024)(128)(4,1)S(1)}, s32[]{:S(2)}) async-start(s8[4718592]{0:T(1024)(128)(4,1)} %bitcast.82), calls=%async_computation.17 | async-start | bytes 8388608
  688.8 6.4 copy-start.29
  688.8 6.4 slice-start.11
  695.2 6.4 copy-start.35
  695.3 6.4 copy-start.37
  704.2 125.4 %copy-start.52 = (f32[768]{0:T(1024)S(1)}, f32[768]{0:T(1024)}, u32[]{:S(2)}) copy-start(f32[768]{0:T(1024)} %copy-done.51) | copy-start | bytes 9220
  704.2 125.4 %copy-start.54 = (f32[768]{0:T(1024)S(1)}, f32[768]{0:T(1024)}, u32[]{:S(2)}) copy-start(f32[768]{0:T(1024)} %get-tuple-element.68) | copy-start | bytes 9220
  829.8 5.9 collective-permute-start.4
  840.9 6.8 collective-permute-start.5
  (45 other events, 172.8 us)
Sparse Core Ops, SparseCore 0:
  62.6 132.2 all-gather.2
  339.3 84.1 reduce-scatter.2
  498.0 89.9 all-gather.4
  667.4 159.7 reduce-scatter.4
  867.1 591.6 all-reduce.5
